TPU v7x, 32 devices: a whole 2x2x4 slice. The times are simulated.
32 devices in a mesh: side: 2 (over core), dom: 16 (over z, y, x).
Axes of the slice: x: 2, y: 2, z: 4, core: 2. Of those that a mesh axis runs over, the one named last changes fastest.
Arguments:
- features: bfloat16 [2, 4096, 1024], P('side', 'dom'), may hold values from -6 to 6
- live_rows: int32 [2, 16], P('side', 'dom'), may hold values from 128 to 256, as said below
- listed: int32 [2, 16, 8, 2], P('side', 'dom'), may hold values from 0 to 1, as said below
- counts: int32 [2, 4096, 2048], P('side', 'dom'), may hold values from 0 to 3, as said below
- cotangent: bfloat16 [2, 4096, 1024], P('side', 'dom'), may hold values from -6 to 6
- q_weight: bfloat16 [1024, 2048], replicated, may hold values from -0.1875 to 0.1875
- q_bias: float32 [2048], replicated, may hold values from -3 to 3
- self_weight: bfloat16 [1024, 1024], replicated, may hold values from -0.109375 to 0.109375
- nb_weight: bfloat16 [2048, 1024], replicated, may hold values from -0.109375 to 0.109375
- out_bias: float32 [1024], replicated, may hold values from -3 to 3
Outputs:
- embedded: bfloat16 [2, 4096, 1024], P('side', 'dom')
- grad_features: bfloat16 [2, 4096, 1024], P('side', 'dom')
Inputs may be any that keep to these rules, and one draw needn't show every extreme that they name: `live_rows`: live rows come first on each device; user devices (group 0) hold one half to three quarters of 256 live rows, item devices three quarters to all. listed[s, j, o, b] is 1 when device (s, j) reads block b of device (1 - s, j - o), positions taken modulo the devices of a group; every block is read by 2 to 4 of the 8 devices that may read it; a device reads at most 1 block of one source, and in every draw some device reads exactly 1 block of some source. `counts`: mostly zero.
All inputs are finite; a program needn't handle non-finite values.
Results may differ from a plain program's by a relative error of at most 0.028.
The roundings to bfloat16 on the way count: a program that leaves them out, or rounds other values in their place, can miss the bound.
Values may be sent and summed in bfloat16 or wider, within the bound.
A program may use at most 128 MiB of HBM per device.

v0:
```python
import jax
import jax.numpy as jnp
from jax import lax
from jax.sharding import PartitionSpec as P

epsilon = 1e-06


def partner_2(block, axis, stride):
    count = lax.axis_size(axis)
    route = []
    for low in range(count):
        high = low | 1 << stride
        if high != low and high < count:
            route += [(low, high), (high, low)]
    return lax.ppermute(block, axis, route)


def shifted(value, axis, steps):
    count = lax.axis_size(axis)
    pairs = [(source, (source + steps) % count) for source in range(count)]
    return lax.ppermute(value, axis, pairs)


def neighbour_rows(features, live_count, q_weight, q_bias):
    row_count = features.shape[0]
    pre_act = jnp.dot(features, q_weight, preferred_element_type=jnp.float32) + q_bias
    keep_rows = (jnp.arange(row_count, dtype=jnp.int32) < live_count)[:, None]
    message = jnp.where(keep_rows, jnp.maximum(pre_act, 0.0), 0.0).astype(jnp.bfloat16)
    return (pre_act, message)


def tile_weights(table, lists, source_live):
    reach, block_count = lists.shape
    row_count = table.shape[0]
    block_rows = row_count // block_count
    listed_cols = jnp.repeat(lists, block_rows, axis=1)
    living = (jnp.arange(row_count, dtype=jnp.int32)[None, :] < source_live[:, None]).astype(
        jnp.int32
    )
    chosen = (listed_cols * living).reshape(1, reach * row_count)
    return (table * chosen).astype(jnp.float32).astype(jnp.bfloat16)


def layer_forward(features, live_count, weight_tiles, messages, self_weight, nb_weight, out_bias):
    row_count = features.shape[0]
    degree = 1.0 + jnp.sum(weight_tiles.astype(jnp.float32), axis=1, keepdims=True)
    summed = jnp.dot(
        weight_tiles, messages.reshape(-1, messages.shape[-1]), preferred_element_type=jnp.float32
    )
    pooled = (summed / degree).astype(jnp.bfloat16)
    pre_act = jnp.dot(features, self_weight, preferred_element_type=jnp.float32)
    pre_act = pre_act + jnp.dot(pooled, nb_weight, preferred_element_type=jnp.float32) + out_bias
    activated = jnp.maximum(pre_act, 0.0)
    inv_norm = lax.rsqrt(jnp.mean(activated * activated, axis=1, keepdims=True) + epsilon)
    keep_rows = (jnp.arange(row_count, dtype=jnp.int32) < live_count)[:, None]
    embedded = jnp.where(keep_rows, activated * inv_norm, 0.0).astype(jnp.bfloat16)
    return (embedded, pre_act, activated, inv_norm, degree, keep_rows)


def layer_backward(
    cotangent, keep_rows, pre_act, activated, inv_norm, degree, self_weight, nb_weight
):
    width = activated.shape[1]
    upstream = jnp.where(keep_rows, cotangent.astype(jnp.float32), 0.0)
    inner = jnp.sum(upstream * activated, axis=1, keepdims=True) / width
    grad_act = inv_norm * upstream - activated * inv_norm * inv_norm * inv_norm * inner
    grad_pre = jnp.where(pre_act > 0, grad_act, 0.0).astype(jnp.bfloat16)
    contract = (((1,), (1,)), ((), ()))
    grad_self = lax.dot_general(grad_pre, self_weight, contract, preferred_element_type=jnp.float32)
    grad_nb = lax.dot_general(grad_pre, nb_weight, contract, preferred_element_type=jnp.float32)
    grad_pooled = (grad_nb / degree).astype(jnp.bfloat16)
    return (grad_self, grad_pooled)


def finish_owner(grad_message, keep_rows, neighbour_pre, grad_self, q_weight):
    grad_neighbour = jnp.where(keep_rows & (neighbour_pre > 0), grad_message, 0.0).astype(
        jnp.bfloat16
    )
    contract = (((1,), (1,)), ((), ()))
    total = grad_self + lax.dot_general(
        grad_neighbour, q_weight, contract, preferred_element_type=jnp.float32
    )
    return jnp.where(keep_rows, total, 0.0).astype(jnp.bfloat16)


def block_slots(row_flags):
    block_count = row_flags.shape[0]
    most = (block_count + 1) // 2
    before = jnp.cumsum(row_flags) - 1
    slot_ids = jnp.arange(most, dtype=jnp.int32)[:, None]
    hits = (row_flags[None, :] == 1) & (before[None, :] == slot_ids)
    chosen = jnp.sum(
        hits.astype(jnp.int32) * jnp.arange(block_count, dtype=jnp.int32)[None, :], axis=1
    )
    return (chosen, jnp.any(hits, axis=1))


def local(
    features,
    live_rows,
    listed,
    counts,
    cotangent,
    q_weight,
    q_bias,
    self_weight,
    nb_weight,
    out_bias,
):
    own_rows = features[0]
    own_live = live_rows[0, 0]
    lists = listed[0, 0]
    table = counts[0]
    upstream = cotangent[0]
    row_count, width = own_rows.shape
    hidden = q_weight.shape[1]
    reach, block_count = lists.shape
    block_rows = row_count // block_count
    levels = reach.bit_length() - 1
    neighbour_pre, message = neighbour_rows(own_rows, own_live, q_weight, q_bias)
    live_vector = live_rows.reshape(1)
    partner, partner_live = partner_2((message, live_vector), "side", 0)
    carried = partner.shape[1]
    lists_window = listed[0]
    for depth_level in range(levels):
        fetched = shifted(lists_window, "dom", -(1 << depth_level))
        lists_window = jnp.concatenate([lists_window, fetched], axis=0)
    partner_blocks = partner.reshape(block_count, block_rows, carried)
    sender_slots = []
    reader_slots = []
    pieces = [partner]
    lives = [partner_live]
    for offset in range(1, reach):
        target_row = lists_window[offset][offset]
        send_block, send_valid = block_slots(target_row)
        sender_slots.append((send_block, send_valid))
        packed = jnp.where(send_valid[:, None, None], partner_blocks[send_block], 0)
        arrived, arrived_live = shifted((packed, partner_live), "dom", offset)
        take_block, take_valid = block_slots(lists[offset])
        reader_slots.append((take_block, take_valid))
        cleaned = jnp.where(take_valid[:, None, None], arrived, 0)
        placed = jnp.zeros_like(partner_blocks).at[take_block].add(cleaned)
        pieces.append(placed.reshape(row_count, carried))
        lives.append(arrived_live)
    window = jnp.stack(pieces)
    window_live = jnp.concatenate(lives)
    weight_tiles = tile_weights(table, lists, window_live)
    outcome = layer_forward(
        own_rows, own_live, weight_tiles, window, self_weight, nb_weight, out_bias
    )
    embedded, pre_act, activated, inv_norm, degree, keep_rows = outcome
    grad_self, grad_pooled = layer_backward(
        upstream, keep_rows, pre_act, activated, inv_norm, degree, self_weight, nb_weight
    )
    returned = lax.dot_general(
        weight_tiles, grad_pooled, (((0,), (0,)), ((), ())), preferred_element_type=jnp.float32
    ).reshape(reach, row_count, hidden)
    total = returned[0].reshape(block_count, block_rows, hidden)
    for offset in range(1, reach):
        take_block, take_valid = reader_slots[offset - 1]
        own_part = returned[offset].reshape(block_count, block_rows, hidden)[take_block]
        packed = jnp.where(take_valid[:, None, None], own_part, 0.0)
        back = shifted(packed, "dom", -offset)
        send_block, send_valid = sender_slots[offset - 1]
        total = total.at[send_block].add(jnp.where(send_valid[:, None, None], back, 0.0))
    total = total.reshape(row_count, hidden)
    grad_message = partner_2(total, "side", 0)
    grad_rows = finish_owner(grad_message, keep_rows, neighbour_pre, grad_self, q_weight)
    return (embedded[None], grad_rows[None])


def solution(mesh):
    return jax.shard_map(
        local,
        mesh=mesh,
        in_specs=(
            P("side", "dom", None),
            P("side", "dom"),
            P("side", "dom", None, None),
            P("side", "dom", None),
            P("side", "dom", None),
            P(),
            P(),
            P(),
            P(),
            P(),
        ),
        out_specs=(P("side", "dom", None), P("side", "dom", None)),
        check_vma=False,
    )
```

profile of v0, /device:TPU:3, one launch (start us, length us, event | category | flops | bytes accessed | tf_op | source)
XLA Modules:
  0.0 513.1 jit_solution(13505465808035220280)
XLA Ops:
  1.5 5.4 %select_convert_fusion.1 = (bf16[256,2048]{1,0:T(8,128)(2,1)}, f32[256,2048]{1,0:T(8,128)}) fusion(pred[256]{0:T(512)(128)(4,1)S(1)} %iota_compare_fusion.1, f32[2048]{0:T(1024)} %param.44, bf16[1024,2048]{1,0:T(8,128)(2,1)} %param.43, bf16[1,256,1024]{2,1,0:T(8,128)(2,1)} %param.38), kind=kOutput, calls=%fused_computation.10 | convolution fusion | flops 1075838976 | bytes 7872768 | tf_op jit(solution)/shard_map/dot_general | solution.py:27
  16.8 0.7 select_reduce_fusion.1
  18.8 0.7 fusion.39
  27.8 0.8 and_reduce_fusion.12
  28.6 2.5 collective-permute-start.1
  31.1 2.1 collective-permute-start.2
  33.2 2.1 collective-permute-done.1
  35.3 3.8 collective-permute-done.2
  39.0 1.7 collective-permute-start.5
  40.7 3.8 collective-permute-start.6
  44.5 0.8 collective-permute-done.6
  45.3 4.4 collective-permute-done.7
  49.6 5.1 concatenate.66
  54.9 1.9 convert_reduce_fusion
  60.0 0.8 and_reduce_fusion.6
  64.5 0.7 fusion.38
  77.4 0.7 fusion.42
  78.1 0.7 fusion.46
  78.8 0.8 and_reduce_fusion.2
  79.7 4.7 dynamic-slice_select_fusion.7
  84.4 2.0 collective-permute-start.10
  86.4 0.8 and_reduce_fusion
  87.3 1.0 collective-permute-start.12
  88.3 0.8 collective-permute-start.13
  89.1 3.7 collective-permute-start.16
  92.9 5.3 %collective-permute-start.17 = (bf16[1,128,2048]{2,1,0:T(8,128)(2,1)S(1)}, bf16[1,128,2048]{2,1,0:T(8,128)(2,1)S(1)}, u32[]{:S(2)}, u32[]{:S(2)}) collective-permute-start(bf16[1,128,2048]{2,1,0:T(8,128)(2,1)S(1)} %get-tuple-element.375), channel_id=1, source_target_pairs={{0,6},{1,7},{2,8},{3,9},{4,10},{5,11},{6,12},{7,13},{8,14},{9,15},... | collective-permute-start | bytes 1572872 | tf_op jit(solution)/shard_map/ppermute | solution.py:22
  98.2 1.3 select_dynamic-update-slice_fusion.6
  99.6 13.5 %collective-permute-done.12 = bf16[1,128,2048]{2,1,0:T(8,128)(2,1)S(1)} collective-permute-done((bf16[1,128,2048]{2,1,0:T(8,128)(2,1)S(1)}, bf16[1,128,2048]{2,1,0:T(8,128)(2,1)S(1)}, u32[]{:S(2)}, u32[]{:S(2)}) %collective-permute-start.12) | collective-permute-done | bytes 524320 | tf_op jit(solution)/shard_map/ppermute | solution.py:22
  113.1 1.4 select_dynamic-update-slice_fusion.5
  114.5 3.5 collective-permute-done.13
  118.1 1.5 select_dynamic-update-slice_fusion.4
  119.7 1.3 select_dynamic-update-slice_fusion.3
  121.5 1.4 select_dynamic-update-slice_fusion.2
  122.9 77.5 %collective-permute-done.17 = bf16[1,128,2048]{2,1,0:T(8,128)(2,1)S(1)} collective-permute-done((bf16[1,128,2048]{2,1,0:T(8,128)(2,1)S(1)}, bf16[1,128,2048]{2,1,0:T(8,128)(2,1)S(1)}, u32[]{:S(2)}, u32[]{:S(2)}) %collective-permute-start.17) | collective-permute-done | bytes 524320 | tf_op jit(solution)/shard_map/ppermute | solution.py:22
  200.5 1.3 select_dynamic-update-slice_fusion.1
  202.2 1.4 select_dynamic-update-slice_fusion
  203.7 3.2 copy-done.3
  206.9 9.7 %fusion.27 = f32[256,1024]{1,0:T(8,128)} fusion(bf16[2048,1024]{1,0:T(8,128)(2,1)} %param.46, bf16[2048,2048]{1,0:T(8,128)(2,1)} %bitcast.312, s32[1,256,2048]{2,1,0:T(8,128)} %param.41, f32[256]{0:T(256)S(1)} %broadcast_add_fusion, s32[2048]{0:T(1024)S(1)} %broadcast_select_fusion), kind=kOutput, calls=%fused_computation.60 | convolution fusion | flops 3223846912 | bytes 15737856 | tf_op jit(solution)/shard_map/dot_general | solution.py:53
  216.6 2.4 fusion.22
  219.1 12.4 %fusion.32 = f32[2048,2048]{1,0:T(8,128)} fusion(s32[1,256,2048]{2,1,0:T(8,128)} %param.41, s32[2048]{0:T(1024)S(1)} %broadcast_select_fusion, bf16[2048,1024]{1,0:T(8,128)(2,1)} %param.46, f32[256]{0:T(256)S(1)} %broadcast_add_fusion, f32[256,1024]{1,0:T(8,128)S(1)} %get-tuple-element.389, bf16[1,256,1024]{2,1,0:T(8,128)(2,1)} %param.42, ...), kind=kOutput, calls=%fused_computation.78 | convolution fusion | flops 3226992640 | bytes 24653056 | tf_op jit(solution)/shard_map/dot_general | solution.py:156
  231.5 6.4 %fusion.53 = (f32[256,2048]{1,0:T(8,128)S(1)}, f32[256,2048]{1,0:T(8,128)S(1)}, f32[256,2048]{1,0:T(8,128)S(1)}, f32[256,2048]{1,0:T(8,128)S(1)}, f32[256,2048]{...) fusion(f32[2048,2048]{1,0:T(8,128)} %fusion.32), kind=kLoop, calls=%fused_computation.201 | loop fusion | bytes 33554432 | tf_op jit(solution)/shard_map/slice | solution.py:162
  239.3 9.3 %collective-permute-start.20 = (f32[1,128,2048]{2,1,0:T(8,128)S(1)}, f32[1,128,2048]{2,1,0:T(8,128)S(1)}, u32[]{:S(2)}, u32[]{:S(2)}) collective-permute-start(f32[1,128,2048]{2,1,0:T(8,128)S(1)} %dynamic-slice_select_fusion.5), channel_id=1, source_target_pairs={{0,14},{1,15},{2,0},{3,1},{4,2},{5,3},{6,4},{7,5},{8,6},{9,7},{10,... | collective-permute-start | bytes 3145736 | tf_op jit(solution)/shard_map/ppermute | solution.py:22
  248.6 0.8 dynamic-slice_select_fusion.4
  249.4 2.9 collective-permute-start.21
  252.2 0.7 dynamic-slice_select_fusion.3
  253.0 0.7 dynamic-slice_select_fusion.2
  253.7 3.4 collective-permute-start.23
  258.6 36.2 %collective-permute-done.19 = f32[1,128,2048]{2,1,0:T(8,128)S(1)} collective-permute-done((f32[1,128,2048]{2,1,0:T(8,128)S(1)}, f32[1,128,2048]{2,1,0:T(8,128)S(1)}, u32[]{:S(2)}, u32[]{:S(2)}) %collective-permute-start.19) | collective-permute-done | bytes 1048608 | tf_op jit(solution)/shard_map/ppermute | solution.py:22
  294.8 1.5 fusion.8
  296.4 32.9 %collective-permute-start.25 = (f32[1,128,2048]{2,1,0:T(8,128)S(1)}, f32[1,128,2048]{2,1,0:T(8,128)S(1)}, u32[]{:S(2)}, u32[]{:S(2)}) collective-permute-start(f32[1,128,2048]{2,1,0:T(8,128)S(1)} %dynamic-slice_select_fusion), channel_id=1, source_target_pairs={{0,9},{1,10},{2,11},{3,12},{4,13},{5,14},{6,15},{7,0},{8,1},{9,2},... | collective-permute-start | bytes 3145736 | tf_op jit(solution)/shard_map/ppermute | solution.py:22
  329.3 1.6 fusion.9
  330.9 1.4 fusion.10
  332.3 1.5 fusion.11
  333.9 2.4 collective-permute-done.23
  336.3 1.5 fusion.12
  337.8 25.4 %collective-permute-done.24 = f32[1,128,2048]{2,1,0:T(8,128)S(1)} collective-permute-done((f32[1,128,2048]{2,1,0:T(8,128)S(1)}, f32[1,128,2048]{2,1,0:T(8,128)S(1)}, u32[]{:S(2)}, u32[]{:S(2)}) %collective-permute-start.24) | collective-permute-done | bytes 1048608 | tf_op jit(solution)/shard_map/ppermute | solution.py:22
  363.2 1.5 fusion.13
  364.7 137.4 %collective-permute-done.25 = f32[1,128,2048]{2,1,0:T(8,128)S(1)} collective-permute-done((f32[1,128,2048]{2,1,0:T(8,128)S(1)}, f32[1,128,2048]{2,1,0:T(8,128)S(1)}, u32[]{:S(2)}, u32[]{:S(2)}) %collective-permute-start.25) | collective-permute-done | bytes 1048608 | tf_op jit(solution)/shard_map/ppermute | solution.py:22
  502.1 1.5 fusion.14
  503.7 3.9 collective-permute-start.26
  507.7 1.0 fusion.29
  508.6 0.9 fusion.51
  509.9 1.0 copy-done.5
  511.0 2.1 fusion.7
  (107 shorter events, 17.8 us)
Async XLA Ops:
  0.6 216.0 %copy-start = (bf16[1024,1024]{1,0:T(8,128)(2,1)S(1)}, bf16[1024,1024]{1,0:T(8,128)(2,1)}, u32[]{:S(2)}) copy-start(bf16[1024,1024]{1,0:T(8,128)(2,1)} %param.45) | copy-start | bytes 6291460
  0.6 56.2 %collective-permute-start.9 = (s32[1,8,2]{1,2,0:T(2,128)}, s32[1,8,2]{1,2,0:T(2,128)S(1)}, u32[]{:S(2)}, u32[]{:S(2)}) collective-permute-start(s32[1,8,2]{1,2,0:T(2,128)} %bitcast.308), channel_id=1, source_target_pairs={{0,15},{1,0},{2,1},{3,2},{4,3},{5,4},{6,5},{7,6},{8,7},{9,8},{10,9... | collective-permute-start | bytes 200 | tf_op jit(solution)/shard_map/ppermute | solution.py:22
  1.5 6.1 %copy-start.2 = (s32[1,1,8,2]{2,3,1,0:T(2,128)S(1)}, s32[1,1,8,2]{2,3,1,0:T(2,128)}, u32[]{:S(2)}) copy-start(s32[1,1,8,2]{2,3,1,0:T(2,128)} %param.40) | copy-start | bytes 196
  1.5 26.3 %copy-start.4 = (s32[3]{0:T(128)S(1)}, s32[3]{0:T(128)}, u32[]{:S(2)}) copy-start(s32[3]{0:T(128)} %constant.348.clone.1) | copy-start | bytes 40
  6.9 72.7 %collective-permute-start.8 = (bf16[256,2048]{1,0:T(8,128)(2,1)}, bf16[256,2048]{1,0:T(8,128)(2,1)S(1)}, u32[]{:S(2)}, u32[]{:S(2)}) collective-permute-start(bf16[256,2048]{1,0:T(8,128)(2,1)} %get-tuple-element.387), channel_id=1, source_target_pairs={{0,16},{16,0},{1,17},{17,1},{2,18},{18,2},{3,19},{19,3},{4,20},{20... | collective-permute-start | bytes 3145736 | tf_op jit(solution)/shard_map/ppermute | solution.py:16
  7.6 21.0 %collective-permute-start = (s32[1]{0:T(128)}, s32[1]{0:T(128)}, u32[]{:S(2)}, u32[]{:S(2)}) collective-permute-start(s32[1]{0:T(128)} %bitcast.2), channel_id=1, source_target_pairs={{0,16},{16,0},{1,17},{17,1},{2,18},{18,2},{3,19},{19,3},{4,20},{20... | collective-permute-start | bytes 20 | tf_op jit(solution)/shard_map/ppermute | solution.py:16
  28.6 6.7 %collective-permute-start.1 = (s32[1]{0:T(128)}, s32[1]{0:T(128)}, u32[]{:S(2)}, u32[]{:S(2)}) collective-permute-start(s32[1]{0:T(128)} %collective-permute-done), channel_id=1, source_target_pairs={{0,1},{1,2},{2,3},{3,4},{4,5},{5,6},{6,7},{7,8},{8,9},{9,10},{10,1... | collective-permute-start | bytes 20 | tf_op jit(solution)/shard_map/ppermute | solution.py:22
  31.1 8.0 %collective-permute-start.2 = (s32[1]{0:T(128)}, s32[1]{0:T(128)}, u32[]{:S(2)}, u32[]{:S(2)}) collective-permute-start(s32[1]{0:T(128)} %collective-permute-done), channel_id=1, source_target_pairs={{0,2},{1,3},{2,4},{3,5},{4,6},{5,7},{6,8},{7,9},{8,10},{9,11},{10,... | collective-permute-start | bytes 20 | tf_op jit(solution)/shard_map/ppermute | solution.py:22
  33.2 7.5 %collective-permute-start.3 = (s32[1]{0:T(128)}, s32[1]{0:T(128)}, u32[]{:S(2)}, u32[]{:S(2)}) collective-permute-start(s32[1]{0:T(128)} %collective-permute-done), channel_id=1, source_target_pairs={{0,3},{1,4},{2,5},{3,6},{4,7},{5,8},{6,9},{7,10},{8,11},{9,12},{10... | collective-permute-start | bytes 20 | tf_op jit(solution)/shard_map/ppermute | solution.py:22
  35.3 9.2 %collective-permute-start.4 = (s32[1]{0:T(128)}, s32[1]{0:T(128)}, u32[]{:S(2)}, u32[]{:S(2)}) collective-permute-start(s32[1]{0:T(128)} %collective-permute-done), channel_id=1, source_target_pairs={{0,4},{1,5},{2,6},{3,7},{4,8},{5,9},{6,10},{7,11},{8,12},{9,13},{1... | collective-permute-start | bytes 20 | tf_op jit(solution)/shard_map/ppermute | solution.py:22
  39.0 5.5 %collective-permute-start.5 = (s32[1]{0:T(128)}, s32[1]{0:T(128)}, u32[]{:S(2)}, u32[]{:S(2)}) collective-permute-start(s32[1]{0:T(128)} %collective-permute-done), channel_id=1, source_target_pairs={{0,5},{1,6},{2,7},{3,8},{4,9},{5,10},{6,11},{7,12},{8,13},{9,14},{... | collective-permute-start | bytes 20 | tf_op jit(solution)/shard_map/ppermute | solution.py:22
  40.7 4.6 collective-permute-start.6
  44.5 5.1 collective-permute-start.7
  59.3 2.5 collective-permute-start.11
  64.4 3.3 collective-permute-start.14
  84.4 8.5 %collective-permute-start.10 = (bf16[1,128,2048]{2,1,0:T(8,128)(2,1)S(1)}, bf16[1,128,2048]{2,1,0:T(8,128)(2,1)S(1)}, u32[]{:S(2)}, u32[]{:S(2)}) collective-permute-start(bf16[1,128,2048]{2,1,0:T(8,128)(2,1)S(1)} %get-tuple-element.380), channel_id=1, source_target_pairs={{0,1},{1,2},{2,3},{3,4},{4,5},{5,6},{6,7},{7,8},{8,9},{9,10},{10,1... | collective-permute-start | bytes 1572872 | tf_op jit(solution)/shard_map/ppermute | solution.py:22
  87.3 25.8 %collective-permute-start.12 = (bf16[1,128,2048]{2,1,0:T(8,128)(2,1)S(1)}, bf16[1,128,2048]{2,1,0:T(8,128)(2,1)S(1)}, u32[]{:S(2)}, u32[]{:S(2)}) collective-permute-start(bf16[1,128,2048]{2,1,0:T(8,128)(2,1)S(1)} %get-tuple-element.379), channel_id=1, source_target_pairs={{0,2},{1,3},{2,4},{3,5},{4,6},{5,7},{6,8},{7,9},{8,10},{9,11},{10,... | collective-permute-start | bytes 1572872 | tf_op jit(solution)/shard_map/ppermute | solution.py:22
  88.3 29.8 %collective-permute-start.13 = (bf16[1,128,2048]{2,1,0:T(8,128)(2,1)S(1)}, bf16[1,128,2048]{2,1,0:T(8,128)(2,1)S(1)}, u32[]{:S(2)}, u32[]{:S(2)}) collective-permute-start(bf16[1,128,2048]{2,1,0:T(8,128)(2,1)S(1)} %get-tuple-element.378), channel_id=1, source_target_pairs={{0,3},{1,4},{2,5},{3,6},{4,7},{5,8},{6,9},{7,10},{8,11},{9,12},{10... | collective-permute-start | bytes 1572872 | tf_op jit(solution)/shard_map/ppermute | solution.py:22
  89.1 30.6 %collective-permute-start.15 = (bf16[1,128,2048]{2,1,0:T(8,128)(2,1)S(1)}, bf16[1,128,2048]{2,1,0:T(8,128)(2,1)S(1)}, u32[]{:S(2)}, u32[]{:S(2)}) collective-permute-start(bf16[1,128,2048]{2,1,0:T(8,128)(2,1)S(1)} %get-tuple-element.377), channel_id=1, source_target_pairs={{0,4},{1,5},{2,6},{3,7},{4,8},{5,9},{6,10},{7,11},{8,12},{9,13},{1... | collective-permute-start | bytes 1572872 | tf_op jit(solution)/shard_map/ppermute | solution.py:22
  89.1 32.3 %collective-permute-start.16 = (bf16[1,128,2048]{2,1,0:T(8,128)(2,1)S(1)}, bf16[1,128,2048]{2,1,0:T(8,128)(2,1)S(1)}, u32[]{:S(2)}, u32[]{:S(2)}) collective-permute-start(bf16[1,128,2048]{2,1,0:T(8,128)(2,1)S(1)} %get-tuple-element.376), channel_id=1, source_target_pairs={{0,5},{1,6},{2,7},{3,8},{4,9},{5,10},{6,11},{7,12},{8,13},{9,14},{... | collective-permute-start | bytes 1572872 | tf_op jit(solution)/shard_map/ppermute | solution.py:22
  92.9 107.5 %collective-permute-start.17 = (bf16[1,128,2048]{2,1,0:T(8,128)(2,1)S(1)}, bf16[1,128,2048]{2,1,0:T(8,128)(2,1)S(1)}, u32[]{:S(2)}, u32[]{:S(2)}) collective-permute-start(bf16[1,128,2048]{2,1,0:T(8,128)(2,1)S(1)} %get-tuple-element.375), channel_id=1, source_target_pairs={{0,6},{1,7},{2,8},{3,9},{4,10},{5,11},{6,12},{7,13},{8,14},{9,15},... | collective-permute-start | bytes 1572872 | tf_op jit(solution)/shard_map/ppermute | solution.py:22
  113.0 89.1 %collective-permute-start.18 = (bf16[1,128,2048]{2,1,0:T(8,128)(2,1)S(1)}, bf16[1,128,2048]{2,1,0:T(8,128)(2,1)S(1)}, u32[]{:S(2)}, u32[]{:S(2)}) collective-permute-start(bf16[1,128,2048]{2,1,0:T(8,128)(2,1)S(1)} %get-tuple-element.374), channel_id=1, source_target_pairs={{0,7},{1,8},{2,9},{3,10},{4,11},{5,12},{6,13},{7,14},{8,15},{9,0},... | collective-permute-start | bytes 1572872 | tf_op jit(solution)/shard_map/ppermute | solution.py:22
  203.7 3.2 copy-start.3
  206.9 9.7 %copy-start.6 = (f32[1024]{0:T(1024)S(1)}, f32[1024]{0:T(1024)}, u32[]{:S(2)}) copy-start(f32[1024]{0:T(1024)} %param.47) | copy-start | bytes 12292
  238.6 56.3 %collective-permute-start.19 = (f32[1,128,2048]{2,1,0:T(8,128)S(1)}, f32[1,128,2048]{2,1,0:T(8,128)S(1)}, u32[]{:S(2)}, u32[]{:S(2)}) collective-permute-start(f32[1,128,2048]{2,1,0:T(8,128)S(1)} %dynamic-slice_select_fusion.6), channel_id=1, source_target_pairs={{0,15},{1,0},{2,1},{3,2},{4,3},{5,4},{6,5},{7,6},{8,7},{9,8},{10,9... | collective-permute-start | bytes 3145736 | tf_op jit(solution)/shard_map/ppermute | solution.py:22
  239.3 57.1 %collective-permute-start.20 = (f32[1,128,2048]{2,1,0:T(8,128)S(1)}, f32[1,128,2048]{2,1,0:T(8,128)S(1)}, u32[]{:S(2)}, u32[]{:S(2)}) collective-permute-start(f32[1,128,2048]{2,1,0:T(8,128)S(1)} %dynamic-slice_select_fusion.5), channel_id=1, source_target_pairs={{0,14},{1,15},{2,0},{3,1},{4,2},{5,3},{6,4},{7,5},{8,6},{9,7},{10,... | collective-permute-start | bytes 3145736 | tf_op jit(solution)/shard_map/ppermute | solution.py:22
  249.4 81.5 %collective-permute-start.21 = (f32[1,128,2048]{2,1,0:T(8,128)S(1)}, f32[1,128,2048]{2,1,0:T(8,128)S(1)}, u32[]{:S(2)}, u32[]{:S(2)}) collective-permute-start(f32[1,128,2048]{2,1,0:T(8,128)S(1)} %dynamic-slice_select_fusion.4), channel_id=1, source_target_pairs={{0,13},{1,14},{2,15},{3,0},{4,1},{5,2},{6,3},{7,4},{8,5},{9,6},{10... | collective-permute-start | bytes 3145736 | tf_op jit(solution)/shard_map/ppermute | solution.py:22
  253.0 79.4 %collective-permute-start.22 = (f32[1,128,2048]{2,1,0:T(8,128)S(1)}, f32[1,128,2048]{2,1,0:T(8,128)S(1)}, u32[]{:S(2)}, u32[]{:S(2)}) collective-permute-start(f32[1,128,2048]{2,1,0:T(8,128)S(1)} %dynamic-slice_select_fusion.3), channel_id=1, source_target_pairs={{0,12},{1,13},{2,14},{3,15},{4,0},{5,1},{6,2},{7,3},{8,4},{9,5},{1... | collective-permute-start | bytes 3145736 | tf_op jit(solution)/shard_map/ppermute | solution.py:22
  253.7 82.5 %collective-permute-start.23 = (f32[1,128,2048]{2,1,0:T(8,128)S(1)}, f32[1,128,2048]{2,1,0:T(8,128)S(1)}, u32[]{:S(2)}, u32[]{:S(2)}) collective-permute-start(f32[1,128,2048]{2,1,0:T(8,128)S(1)} %dynamic-slice_select_fusion.2), channel_id=1, source_target_pairs={{0,11},{1,12},{2,13},{3,14},{4,15},{5,0},{6,1},{7,2},{8,3},{9,4},{... | collective-permute-start | bytes 3145736 | tf_op jit(solution)/shard_map/ppermute | solution.py:22
  294.8 68.3 %collective-permute-start.24 = (f32[1,128,2048]{2,1,0:T(8,128)S(1)}, f32[1,128,2048]{2,1,0:T(8,128)S(1)}, u32[]{:S(2)}, u32[]{:S(2)}) collective-permute-start(f32[1,128,2048]{2,1,0:T(8,128)S(1)} %dynamic-slice_select_fusion.1), channel_id=1, source_target_pairs={{0,10},{1,11},{2,12},{3,13},{4,14},{5,15},{6,0},{7,1},{8,2},{9,3},... | collective-permute-start | bytes 3145736 | tf_op jit(solution)/shard_map/ppermute | solution.py:22
  296.4 205.7 %collective-permute-start.25 = (f32[1,128,2048]{2,1,0:T(8,128)S(1)}, f32[1,128,2048]{2,1,0:T(8,128)S(1)}, u32[]{:S(2)}, u32[]{:S(2)}) collective-permute-start(f32[1,128,2048]{2,1,0:T(8,128)S(1)} %dynamic-slice_select_fusion), channel_id=1, source_target_pairs={{0,9},{1,10},{2,11},{3,12},{4,13},{5,14},{6,15},{7,0},{8,1},{9,2},... | collective-permute-start | bytes 3145736 | tf_op jit(solution)/shard_map/ppermute | solution.py:22
  503.6 5.0 copy-start.1
  503.7 6.2 %collective-permute-start.26 = (bf16[256,2048]{1,0:T(8,128)(2,1)S(1)}, bf16[256,2048]{1,0:T(8,128)(2,1)S(1)}, u32[]{:S(2)}, u32[]{:S(2)}) collective-permute-start(bf16[256,2048]{1,0:T(8,128)(2,1)S(1)} %bitcast_convert_fusion), channel_id=1, source_target_pairs={{0,16},{16,0},{1,17},{17,1},{2,18},{18,2},{3,19},{19,3},{4,20},{20... | collective-permute-start | bytes 3145736 | tf_op jit(solution)/shard_map/ppermute | solution.py:16
  507.7 2.3 copy-start.7
  508.6 2.3 copy-start.5
where the time goes:
time: 514 us; the launch traced here: 513 us
  waiting for transfers between devices  308 us (60%)
  starting transfers between devices  76.3 us (15%)
  other arithmetic  50.3 us (10%)
  matrix products  32.9 us (6%)
  between operations  27.7 us (5%)
  local copies, waits for them, and re-layouts  18.3 us (4%)
    ppermute x24, waiting for transfers between devices, shifted(): return lax.ppermute(value, axis, pairs)  307 us
    ppermute x24, starting transfers between devices, shifted(): return lax.ppermute(value, axis, pairs)  71.7 us
    dot_general x1, matrix products, local(): lax.dot_general(weight_tiles, grad_pooled, (((0,), (0,)), ((), ())), pref...  12.4 us
    scatter-add x7, other arithmetic, local(): total.at[send_block].add(jnp.where(send_valid[:, None, None], back, 0.0))  10.6 us
  transfers between devices with their start and end apart: 27, of which 13 were waited for; matrix products, arithmetic and copies ran while one was open for 11% of the time, Pallas kernels for 0%

commit v1 on v0

v1 whole, which is shorter than its diff:
```python
import functools

import jax
import jax.numpy as jnp
from jax import lax
from jax.experimental import pallas as pl
from jax.experimental.pallas import tpu as pltpu
from jax.sharding import PartitionSpec as P

MESH = pl.DeviceIdType.MESH
epsilon = 1e-06
f32 = jnp.float32
bf16 = jnp.bfloat16
NT = (((1,), (1,)), ((), ()))


def tile_of(extent, most=512):
    return most if extent % most == 0 else extent


def kernel(
    reach,
    group,
    lists,
    live,
    meta,
    feats,
    q_bias,
    out_bias,
    counts_hbm,
    cot_hbm,
    q_hbm,
    self_hbm,
    nb_hbm,
    embedded,
    grads,
    counts,
    cot,
    q,
    selfw,
    nb,
    reader_meta,
    source_meta,
    send_f,
    recv_f,
    send_b,
    recv_b,
    tiles,
    tiles_t,
    degree,
    messages,
    acc,
    pre_act,
    grad_pre,
    grad_pooled,
    masked,
    total,
    load_sems,
    meta_s,
    meta_r,
    live_s,
    live_r,
    fs,
    fr,
    bs,
    br,
):
    rows, width = feats.shape
    hidden = q.shape[1]
    block = recv_f.shape[0] // reach
    pair = 2 * block
    side = lax.axis_index("side")
    me = lax.axis_index("dom")
    other = 1 - side

    def reader(offset):
        return (other, lax.rem(me + offset, group))

    def source(offset):
        return (other, lax.rem(me + group - offset, group))

    loads = [
        pltpu.make_async_copy(src, dst, load_sems.at[at])
        for at, (src, dst) in enumerate(
            (
                (counts_hbm, counts),
                (q_hbm, q),
                (self_hbm, selfw),
                (nb_hbm, nb),
                (cot_hbm, cot),
            )
        )
    ]
    for load in loads:
        load.start()

    barrier = pltpu.get_barrier_semaphore()

    def greet(offset, _):
        pl.semaphore_signal(barrier, inc=1, device_id=reader(offset), device_id_type=MESH)
        return _

    def greet_back(offset, _):
        pl.semaphore_signal(barrier, inc=1, device_id=source(offset), device_id_type=MESH)
        return _

    lax.fori_loop(0, reach, greet, 0)
    lax.fori_loop(1, reach, greet_back, 0)
    pl.semaphore_wait(barrier, 2 * reach - 1)

    def meta_copy(offset):
        return pltpu.make_async_remote_copy(
            src_ref=meta.at[offset],
            dst_ref=reader_meta.at[offset],
            send_sem=meta_s.at[offset],
            recv_sem=meta_r.at[offset],
            device_id=source(offset),
            device_id_type=MESH,
        )

    def live_copy(offset):
        return pltpu.make_async_remote_copy(
            src_ref=meta.at[offset],
            dst_ref=source_meta.at[offset],
            send_sem=live_s.at[offset],
            recv_sem=live_r.at[offset],
            device_id=reader(offset),
            device_id_type=MESH,
        )

    def block_rows(offset):
        return pl.ds(pl.multiple_of(offset * block, block), block)

    def forward_copy(offset):
        return pltpu.make_async_remote_copy(
            src_ref=send_f.at[block_rows(offset)],
            dst_ref=recv_f.at[block_rows(offset)],
            send_sem=fs.at[offset],
            recv_sem=fr.at[offset],
            device_id=reader(offset),
            device_id_type=MESH,
        )

    def backward_copy(offset):
        return pltpu.make_async_remote_copy(
            src_ref=send_b.at[block_rows(offset)],
            dst_ref=recv_b.at[block_rows(offset)],
            send_sem=bs.at[offset],
            recv_sem=br.at[offset],
            device_id=source(offset),
            device_id_type=MESH,
        )

    def start_meta(step, _):
        offset = reach - 1 - step
        meta_copy(offset).start()
        return _

    def start_live(step, _):
        live_copy(reach - 1 - step).start()
        return _

    lax.fori_loop(0, reach, start_meta, 0)
    lax.fori_loop(0, reach, start_live, 0)

    def second_wanted(offset):
        lane = reader_meta[offset][1:2, :]
        return jnp.concatenate([lane] * (width // lane.shape[1]), axis=1)

    def send_features(step, _):
        offset = reach - 1 - step
        meta_copy(offset).wait_recv()
        flag = second_wanted(offset)
        first = feats[:block, :].astype(f32)
        second = feats[block:, :].astype(f32)
        send_f[block_rows(offset), :] = (first * (1.0 - flag) + second * flag).astype(bf16)
        forward_copy(offset).start()
        return _

    lax.fori_loop(0, reach, send_features, 0)

    loads[0].wait()
    acc[...] = jnp.zeros_like(acc)
    lanes = meta.shape[2]
    column = lax.broadcasted_iota(jnp.int32, (1, lanes), 1).astype(f32)
    degree[...] = jnp.zeros_like(degree)

    def build(offset, _):
        live_copy(offset).wait_recv()
        source_live = source_meta[offset][2:3, :]
        at = pl.multiple_of(offset * rows, block)
        weight_0 = jnp.where(column < source_live, meta[offset][0:1, :], 0.0)
        weight_1 = jnp.where(column + block < source_live, meta[offset][1:2, :], 0.0)
        tile = counts[:, pl.ds(at, block)].astype(f32) * weight_0
        tile = tile + counts[:, pl.ds(pl.multiple_of(at + block, block), block)].astype(f32) * weight_1
        degree[...] += tile
        tiles[:, block_rows(offset)] = tile.astype(bf16)
        tiles_t[block_rows(offset), :] = tile.T.astype(bf16)
        return _

    lax.fori_loop(0, reach, build, 0)
    row_degree = 1.0 + jnp.sum(degree[...], axis=1, keepdims=True)
    degree[...] = jnp.broadcast_to(row_degree, degree.shape)

    wide = tile_of(width)
    deep = tile_of(hidden)

    def columns(step, size):
        return pl.ds(pl.multiple_of(step * size, size), size)

    loads[2].wait()

    def own_part(step, _):
        at = columns(step, wide)
        pre_act[:, at] = jnp.dot(feats[...], selfw[:, at], preferred_element_type=f32) + out_bias[:, at]
        return _

    lax.fori_loop(0, width // wide, own_part, 0)
    loads[1].wait()

    def pool(step, _):
        chosen = reach // 2 - 1 - step
        forward_copy(2 * chosen).wait_recv()
        forward_copy(2 * chosen + 1).wait_recv()
        here = columns(chosen, pair)

        def part(inner, _):
            at = columns(inner, deep)
            pre = jnp.dot(recv_f[here, :], q[:, at], preferred_element_type=f32) + q_bias[:, at]
            message = jnp.maximum(pre, 0.0).astype(bf16)
            messages[here, at] = message
            acc[:, at] += jnp.dot(tiles[:, here], message, preferred_element_type=f32)
            return _

        return lax.fori_loop(0, hidden // deep, part, _)

    lax.fori_loop(0, reach // 2, pool, 0)

    def over_degree(value):
        lane = degree[...]
        return value / jnp.concatenate([lane] * (value.shape[1] // lane.shape[1]), axis=1)

    def scale(step, _):
        at = columns(step, deep)
        grad_pooled[:, at] = over_degree(acc[:, at]).astype(bf16)
        return _

    lax.fori_loop(0, hidden // deep, scale, 0)
    loads[3].wait()

    def add_pooled(step, _):
        at = columns(step, wide)
        pre_act[:, at] += jnp.dot(grad_pooled[...], nb[:, at], preferred_element_type=f32)
        return _

    lax.fori_loop(0, width // wide, add_pooled, 0)
    loads[4].wait()
    own_live = live[0, 0]
    chunk = 32

    def normalise(step, _):
        here = columns(step, chunk)
        pre = pre_act[here, :]
        keep = (lax.broadcasted_iota(jnp.int32, (chunk, 1), 0) + step * chunk) < own_live
        activated = jnp.maximum(pre, 0.0)
        mean = jnp.sum(activated * activated, axis=1, keepdims=True) / width
        inv_norm = lax.rsqrt(mean + epsilon)
        embedded[here, :] = jnp.where(keep, activated * inv_norm, 0.0).astype(bf16)
        upstream = jnp.where(keep, cot[here, :].astype(f32), 0.0)
        inner = jnp.sum(upstream * activated, axis=1, keepdims=True) / width
        grad_act = inv_norm * upstream - activated * (inv_norm * inv_norm * inv_norm * inner)
        grad_pre[here, :] = jnp.where(pre > 0, grad_act, 0.0).astype(bf16)
        return _

    lax.fori_loop(0, rows // chunk, normalise, 0)

    def pooled_gradient(step, _):
        at = columns(step, deep)
        value = lax.dot_general(grad_pre[...], nb[at, :], NT, preferred_element_type=f32)
        grad_pooled[:, at] = over_degree(value).astype(bf16)
        return _

    lax.fori_loop(0, hidden // deep, pooled_gradient, 0)

    def send_back(step, _):
        chosen = reach // 2 - 1 - step
        here = columns(chosen, pair)

        def mask(inner, _):
            at = columns(inner, deep)
            value = jnp.dot(tiles_t[here, :], grad_pooled[:, at], preferred_element_type=f32)
            masked[:, at] = jnp.where(messages[here, at].astype(f32) > 0, value, 0.0).astype(bf16)
            return _

        lax.fori_loop(0, hidden // deep, mask, 0)

        def project(inner, _):
            at = columns(inner, wide)
            value = lax.dot_general(masked[...], q[at, :], NT, preferred_element_type=f32)
            send_b[here, at] = value.astype(bf16)
            return _

        lax.fori_loop(0, width // wide, project, 0)
        backward_copy(2 * chosen + 1).start()
        backward_copy(2 * chosen).start()
        return _

    lax.fori_loop(0, reach // 2, send_back, 0)

    def own_gradient(step, _):
        at = columns(step, wide)
        total[:, at] = lax.dot_general(grad_pre[...], selfw[at, :], NT, preferred_element_type=f32)
        return _

    lax.fori_loop(0, width // wide, own_gradient, 0)

    def collect(step, _):
        offset = reach - 1 - step
        backward_copy(offset).wait_recv()
        flag = second_wanted(offset)
        arrived = recv_b[block_rows(offset), :].astype(f32)
        total[:block, :] += arrived * (1.0 - flag)
        total[block:, :] += arrived * flag
        return _

    lax.fori_loop(0, reach, collect, 0)

    def finish(step, _):
        here = columns(step, chunk)
        keep = (lax.broadcasted_iota(jnp.int32, (chunk, 1), 0) + step * chunk) < own_live
        grads[here, :] = jnp.where(keep, total[here, :], 0.0).astype(bf16)
        return _

    lax.fori_loop(0, rows // chunk, finish, 0)

    def drain(offset, _):
        meta_copy(offset).wait_send()
        live_copy(offset).wait_send()
        forward_copy(offset).wait_send()
        backward_copy(offset).wait_send()
        return _

    lax.fori_loop(0, reach, drain, 0)


def solution(mesh):
    group = mesh.shape["dom"]

    def local(
        features,
        live_rows,
        listed,
        counts,
        cotangent,
        q_weight,
        q_bias,
        self_weight,
        nb_weight,
        out_bias,
    ):
        rows, width = features.shape[1:]
        hidden = q_weight.shape[1]
        reach, block_count = listed.shape[2:]
        block = rows // block_count
        lists = listed[0, 0]
        lane = 128
        flags = lists.astype(f32)
        live = jnp.broadcast_to(live_rows.astype(f32).reshape(1, 1), (reach, 1))
        columns = jnp.concatenate([flags, live, jnp.zeros((reach, 8 - block_count - 1), f32)], axis=1)
        meta = jnp.broadcast_to(columns[:, :, None], (reach, 8, lane))
        vmem = pl.BlockSpec(memory_space=pltpu.VMEM)
        smem = pl.BlockSpec(memory_space=pltpu.SMEM)
        hbm = pl.BlockSpec(memory_space=pl.ANY)
        dma = pltpu.SemaphoreType.DMA((reach,))
        embedded, grads = pl.pallas_call(
            functools.partial(kernel, reach, group),
            out_shape=(
                jax.ShapeDtypeStruct((rows, width), bf16),
                jax.ShapeDtypeStruct((rows, width), bf16),
            ),
            in_specs=[smem, smem, vmem, vmem, vmem, vmem, hbm, hbm, hbm, hbm, hbm],
            out_specs=(vmem, vmem),
            scratch_shapes=[
                pltpu.VMEM((rows, reach * rows), jnp.int32),
                pltpu.VMEM((rows, width), bf16),
                pltpu.VMEM((width, hidden), bf16),
                pltpu.VMEM((width, width), bf16),
                pltpu.VMEM((hidden, width), bf16),
                pltpu.VMEM((reach, 8, lane), f32),
                pltpu.VMEM((reach, 8, lane), f32),
                pltpu.VMEM((reach * block, width), bf16),
                pltpu.VMEM((reach * block, width), bf16),
                pltpu.VMEM((reach * block, width), bf16),
                pltpu.VMEM((reach * block, width), bf16),
                pltpu.VMEM((rows, reach * block), bf16),
                pltpu.VMEM((reach * block, rows), bf16),
                pltpu.VMEM((rows, block), f32),
                pltpu.VMEM((reach * block, hidden), bf16),
                pltpu.VMEM((rows, hidden), f32),
                pltpu.VMEM((rows, width), f32),
                pltpu.VMEM((rows, width), bf16),
                pltpu.VMEM((rows, hidden), bf16),
                pltpu.VMEM((2 * block, hidden), bf16),
                pltpu.VMEM((rows, width), f32),
                pltpu.SemaphoreType.DMA((5,)),
                dma,
                dma,
                dma,
                dma,
                dma,
                dma,
                dma,
                dma,
            ],
            compiler_params=pltpu.CompilerParams(
                collective_id=0, has_side_effects=True, vmem_limit_bytes=60 * 1024 * 1024
            ),
        )(
            lists,
            live_rows,
            meta,
            features[0],
            q_bias.reshape(1, hidden),
            out_bias.reshape(1, width),
            counts[0],
            cotangent[0],
            q_weight,
            self_weight,
            nb_weight,
        )
        return (embedded[None], grads[None])

    return jax.shard_map(
        local,
        mesh=mesh,
        in_specs=(
            P("side", "dom", None),
            P("side", "dom"),
            P("side", "dom", None, None),
            P("side", "dom", None),
            P("side", "dom", None),
            P(),
            P(),
            P(),
            P(),
            P(),
        ),
        out_specs=(P("side", "dom", None), P("side", "dom", None)),
        check_vma=False,
    )
```

time: 514 us -> 159 us (0.31)
  the two profiles are of different devices: /device:TPU:3 before, /device:TPU:15 now
where the time goes in v1:
time: 159 us; the launch traced here: 158 us
  Pallas kernels  150 us (94%)
  local copies, waits for them, and re-layouts  6.01 us (4%)
    pallas_call x1, Pallas kernels, local(): pl.pallas_call(functools.partial(kernel, reach, group), out_shape=(jax.Sh...  150 us
    unnamed x2, local copies, waits for them, and re-layouts  3.74 us

profile of v1, /device:TPU:15, one launch (start us, length us, event | category | flops | bytes accessed | tf_op | source)
XLA Modules:
  0.0 158.5 jit_solution(1142656960265182834)
XLA Ops:
  1.3 0.1 pad.1.clone
  1.4 0.1 pad.2.clone
  1.4 0.7 bitcast_convert_fusion
  2.1 0.1 copy.12
  2.2 1.3 copy.13.lists
  3.6 0.7 broadcast_in_dim.25.meta
  4.2 150.5 %shard_map.113 = (bf16[256,1024]{1,0:T(8,128)(2,1)}, bf16[256,1024]{1,0:T(8,128)(2,1)}) custom-call(s32[8,2]{1,0:T(8,128)} %copy.13.lists, s32[1,1]{1,0:T(1,128)S(6)} %copy.16.live, f32[8,8,128]{2,1,0:T(8,128)} %broadcast_in_dim.25.meta, bf16[256,1024]{1,0:T(8,128)(2,1)} %bitcast.15, f32[1,2048]{1,0:T(1,128)} %bitcast.17, f32[1,1024]{1,0:T(1,128)} %bitcast.18, ...), custom_call_target="tpu_custom_call" | custom-call | tf_op jit(solution)/shard_map/pallas_call | solution.py:375
  154.7 1.9 %copy.17 = bf16[1,256,1024]{2,1,0:T(8,128)(2,1)} copy(bf16[1,256,1024]{2,1,0:T(8,128)(2,1)} %bitcast.14) | data formatting | bytes 1048576
  156.6 1.9 %copy.18 = bf16[1,256,1024]{2,1,0:T(8,128)(2,1)} copy(bf16[1,256,1024]{2,1,0:T(8,128)(2,1)} %bitcast.13) | data formatting | bytes 1048576
  (2 shorter events, 0.0 us)

commit v2 on v1

--- a/solution.py
+++ b/solution.py
@@ -45,6 +45,13 @@
     recv_f,
     send_b,
     recv_b,
+    plane_1,
+    plane_2,
+    up_send_1,
+    up_send_2,
+    up_1,
+    up_2,
+    part_sum,
     tiles,
     tiles_t,
     degree,
@@ -53,7 +60,6 @@
     pre_act,
     grad_pre,
     grad_pooled,
-    masked,
     total,
     load_sems,
     meta_s,
@@ -64,6 +70,14 @@
     fr,
     bs,
     br,
+    z1_s,
+    z1_r,
+    z2_s,
+    z2_r,
+    u1_s,
+    u1_r,
+    u2_s,
+    u2_r,
 ):
     rows, width = feats.shape
     hidden = q.shape[1]
@@ -72,6 +86,18 @@
     side = lax.axis_index("side")
     me = lax.axis_index("dom")
     other = 1 - side
+    ring = reach // 2
+    spot = lax.rem(me, ring)
+    base = me - spot
+    parts, part_width = send_b.shape[0], send_b.shape[2]
+    ahead = (side, lax.rem(me + ring, group))
+    behind = (side, lax.rem(me + group - ring, group))
+
+    def mate(offset):
+        return (other, base + lax.rem(spot + offset, ring))
+
+    def relay(offset):
+        return (other, base + lax.rem(spot + 2 * ring - offset, ring))
 
     def reader(offset):
         return (other, lax.rem(me + offset, group))
@@ -106,7 +132,9 @@
 
     lax.fori_loop(0, reach, greet, 0)
     lax.fori_loop(1, reach, greet_back, 0)
-    pl.semaphore_wait(barrier, 2 * reach - 1)
+    pl.semaphore_signal(barrier, inc=1, device_id=ahead, device_id_type=MESH)
+    pl.semaphore_signal(barrier, inc=1, device_id=behind, device_id_type=MESH)
+    pl.semaphore_wait(barrier, 2 * reach + 1)
 
     def meta_copy(offset):
         return pltpu.make_async_remote_copy(
@@ -114,7 +142,7 @@
             dst_ref=reader_meta.at[offset],
             send_sem=meta_s.at[offset],
             recv_sem=meta_r.at[offset],
-            device_id=source(offset),
+            device_id=relay(offset),
             device_id_type=MESH,
         )
 
@@ -137,19 +165,47 @@
             dst_ref=recv_f.at[block_rows(offset)],
             send_sem=fs.at[offset],
             recv_sem=fr.at[offset],
-            device_id=reader(offset),
+            device_id=mate(offset),
             device_id_type=MESH,
         )
 
-    def backward_copy(offset):
+    def backward_copy(offset, part):
         return pltpu.make_async_remote_copy(
-            src_ref=send_b.at[block_rows(offset)],
-            dst_ref=recv_b.at[block_rows(offset)],
-            send_sem=bs.at[offset],
-            recv_sem=br.at[offset],
-            device_id=source(offset),
+            src_ref=send_b.at[part, block_rows(offset)],
+            dst_ref=recv_b.at[part, block_rows(offset)],
+            send_sem=bs.at[part, offset],
+            recv_sem=br.at[part, offset],
+            device_id=relay(offset),
             device_id_type=MESH,
         )
+
+    def plane_copy(src, dst, send, recv, half):
+        return pltpu.make_async_remote_copy(
+            src_ref=src.at[block_rows(half)],
+            dst_ref=dst.at[block_rows(half)],
+            send_sem=send.at[half],
+            recv_sem=recv.at[half],
+            device_id=ahead,
+            device_id_type=MESH,
+        )
+
+    def up_copy(src, dst, send, recv, part):
+        return pltpu.make_async_remote_copy(
+            src_ref=src.at[part],
+            dst_ref=dst.at[part],
+            send_sem=send.at[part],
+            recv_sem=recv.at[part],
+            device_id=behind,
+            device_id_type=MESH,
+        )
+
+    halves = rows // block
+    to_next = [plane_copy(feats, plane_1, z1_s, z1_r, half) for half in range(halves)]
+    to_second = [plane_copy(plane_1, plane_2, z2_s, z2_r, half) for half in range(halves)]
+    first_up = [up_copy(up_send_1, up_1, u1_s, u1_r, part) for part in range(parts)]
+    second_up = [up_copy(up_send_2, up_2, u2_s, u2_r, part) for part in range(parts)]
+    for copy in to_next:
+        copy.start()
 
     def start_meta(step, _):
         offset = reach - 1 - step
@@ -163,21 +219,31 @@
     lax.fori_loop(0, reach, start_meta, 0)
     lax.fori_loop(0, reach, start_live, 0)
 
-    def second_wanted(offset):
+    def second_wanted(offset, size):
         lane = reader_meta[offset][1:2, :]
-        return jnp.concatenate([lane] * (width // lane.shape[1]), axis=1)
-
-    def send_features(step, _):
-        offset = reach - 1 - step
-        meta_copy(offset).wait_recv()
-        flag = second_wanted(offset)
-        first = feats[:block, :].astype(f32)
-        second = feats[block:, :].astype(f32)
+        return jnp.concatenate([lane] * (size // lane.shape[1]), axis=1)
+
+    def pack(offset, rows_of):
+        flag = second_wanted(offset, width)
+        first = rows_of[:block, :].astype(f32)
+        second = rows_of[block:, :].astype(f32)
         send_f[block_rows(offset), :] = (first * (1.0 - flag) + second * flag).astype(bf16)
         forward_copy(offset).start()
-        return _
-
-    lax.fori_loop(0, reach, send_features, 0)
+
+    def middle(step):
+        return jnp.where(spot + step < ring, step + ring, step)
+
+    def take_meta(offset, _):
+        meta_copy(offset).wait_recv()
+        return _
+
+    lax.fori_loop(0, reach, take_meta, 0)
+
+    def send_own(step, _):
+        pack(step, feats)
+        return _
+
+    lax.fori_loop(0, ring - spot, send_own, 0)
 
     loads[0].wait()
     acc[...] = jnp.zeros_like(acc)
@@ -202,6 +268,19 @@
     row_degree = 1.0 + jnp.sum(degree[...], axis=1, keepdims=True)
     degree[...] = jnp.broadcast_to(row_degree, degree.shape)
 
+    for first, second in zip(to_next, to_second):
+        first.wait_recv()
+
+        @pl.when(spot > 0)
+        def _():
+            second.start()
+
+    def send_middle(step, _):
+        pack(middle(step), plane_1)
+        return _
+
+    lax.fori_loop(0, ring, send_middle, 0)
+
     wide = tile_of(width)
     deep = tile_of(hidden)
 
@@ -219,7 +298,7 @@
     loads[1].wait()
 
     def pool(step, _):
-        chosen = reach // 2 - 1 - step
+        chosen = step
         forward_copy(2 * chosen).wait_recv()
         forward_copy(2 * chosen + 1).wait_recv()
         here = columns(chosen, pair)
@@ -234,7 +313,19 @@
 
         return lax.fori_loop(0, hidden // deep, part, _)
 
-    lax.fori_loop(0, reach // 2, pool, 0)
+    lax.fori_loop(0, ring // 2, pool, 0)
+
+    @pl.when(spot > 0)
+    def _():
+        for copy in to_second:
+            copy.wait_recv()
+
+    def send_far(step, _):
+        pack(step + ring, plane_2)
+        return _
+
+    lax.fori_loop(ring - spot, ring, send_far, 0)
+    lax.fori_loop(ring // 2, ring, pool, 0)
 
     def over_degree(value):
         lane = degree[...]
@@ -282,30 +373,39 @@
 
     lax.fori_loop(0, hidden // deep, pooled_gradient, 0)
 
-    def send_back(step, _):
+    def mask(step, _):
         chosen = reach // 2 - 1 - step
         here = columns(chosen, pair)
 
-        def mask(inner, _):
+        def inner_mask(inner, _):
             at = columns(inner, deep)
             value = jnp.dot(tiles_t[here, :], grad_pooled[:, at], preferred_element_type=f32)
-            masked[:, at] = jnp.where(messages[here, at].astype(f32) > 0, value, 0.0).astype(bf16)
+            messages[here, at] = jnp.where(messages[here, at].astype(f32) > 0, value, 0.0).astype(bf16)
             return _
 
-        lax.fori_loop(0, hidden // deep, mask, 0)
-
-        def project(inner, _):
-            at = columns(inner, wide)
-            value = lax.dot_general(masked[...], q[at, :], NT, preferred_element_type=f32)
-            send_b[here, at] = value.astype(bf16)
-            return _
-
-        lax.fori_loop(0, width // wide, project, 0)
-        backward_copy(2 * chosen + 1).start()
-        backward_copy(2 * chosen).start()
-        return _
-
-    lax.fori_loop(0, reach // 2, send_back, 0)
+        return lax.fori_loop(0, hidden // deep, inner_mask, _)
+
+    def project(part, step):
+        chosen = reach // 2 - 1 - step
+        here = columns(chosen, pair)
+        at = columns(part, part_width)
+        value = lax.dot_general(messages[here, :], q[at, :], NT, preferred_element_type=f32)
+        send_b[part, here, :] = value.astype(bf16)
+        backward_copy(2 * chosen + 1, part).start()
+        backward_copy(2 * chosen, part).start()
+
+    def first_back(step, _):
+        mask(step, 0)
+        project(0, step)
+        return _
+
+    lax.fori_loop(0, reach // 2, first_back, 0)
+
+    def later_back(step, _):
+        project(1 + step // (reach // 2), lax.rem(step, reach // 2))
+        return _
+
+    lax.fori_loop(0, (parts - 1) * (reach // 2), later_back, 0)
 
     def own_gradient(step, _):
         at = columns(step, wide)
@@ -314,16 +414,55 @@
 
     lax.fori_loop(0, width // wide, own_gradient, 0)
 
-    def collect(step, _):
-        offset = reach - 1 - step
-        backward_copy(offset).wait_recv()
-        flag = second_wanted(offset)
-        arrived = recv_b[block_rows(offset), :].astype(f32)
-        total[:block, :] += arrived * (1.0 - flag)
-        total[block:, :] += arrived * flag
-        return _
-
-    lax.fori_loop(0, reach, collect, 0)
+    def collect(offset, part, target):
+        backward_copy(offset, part).wait_recv()
+        flag = second_wanted(offset, part_width)
+        arrived = recv_b[part, block_rows(offset), :].astype(f32)
+        target[:block, :] += arrived * (1.0 - flag)
+        target[block:, :] += arrived * flag
+
+    for part in range(parts):
+
+        @pl.when(spot > 0)
+        def _():
+            part_sum[...] = jnp.zeros_like(part_sum)
+
+            def far(step, _):
+                collect(step + ring, part, part_sum)
+                return _
+
+            lax.fori_loop(ring - spot, ring, far, 0)
+            up_send_2[part] = part_sum[...].astype(bf16)
+            second_up[part].start()
+
+        part_sum[...] = jnp.zeros_like(part_sum)
+
+        def near(step, _):
+            collect(middle(step), part, part_sum)
+            return _
+
+        lax.fori_loop(0, ring, near, 0)
+
+        @pl.when(spot > 0)
+        def _():
+            second_up[part].wait_recv()
+            part_sum[...] += up_2[part].astype(f32)
+
+        up_send_1[part] = part_sum[...].astype(bf16)
+        first_up[part].start()
+
+    for part in range(parts):
+        view = total.at[:, pl.ds(part * part_width, part_width)]
+
+        def own(step, _):
+            collect(step, part, view)
+            return _
+
+        lax.fori_loop(0, ring - spot, own, 0)
+
+    for part in range(parts):
+        first_up[part].wait_recv()
+        total[:, pl.ds(part * part_width, part_width)] += up_1[part].astype(f32)
 
     def finish(step, _):
         here = columns(step, chunk)
@@ -337,10 +476,18 @@
         meta_copy(offset).wait_send()
         live_copy(offset).wait_send()
         forward_copy(offset).wait_send()
-        backward_copy(offset).wait_send()
+        for part in range(parts):
+            backward_copy(offset, part).wait_send()
         return _
 
     lax.fori_loop(0, reach, drain, 0)
+    for copy in to_next + first_up:
+        copy.wait_send()
+
+    @pl.when(spot > 0)
+    def _():
+        for copy in to_second + second_up:
+            copy.wait_send()
 
 
 def solution(mesh):
@@ -364,6 +511,7 @@
         block = rows // block_count
         lists = listed[0, 0]
         lane = 128
+        parts = 2
         flags = lists.astype(f32)
         live = jnp.broadcast_to(live_rows.astype(f32).reshape(1, 1), (reach, 1))
         columns = jnp.concatenate([flags, live, jnp.zeros((reach, 8 - block_count - 1), f32)], axis=1)
@@ -372,6 +520,9 @@
         smem = pl.BlockSpec(memory_space=pltpu.SMEM)
         hbm = pl.BlockSpec(memory_space=pl.ANY)
         dma = pltpu.SemaphoreType.DMA((reach,))
+        by_part = pltpu.SemaphoreType.DMA((parts, reach))
+        half = pltpu.SemaphoreType.DMA((block_count,))
+        strip = pltpu.SemaphoreType.DMA((parts,))
         embedded, grads = pl.pallas_call(
             functools.partial(kernel, reach, group),
             out_shape=(
@@ -390,8 +541,15 @@
                 pltpu.VMEM((reach, 8, lane), f32),
                 pltpu.VMEM((reach * block, width), bf16),
                 pltpu.VMEM((reach * block, width), bf16),
-                pltpu.VMEM((reach * block, width), bf16),
-                pltpu.VMEM((reach * block, width), bf16),
+                pltpu.VMEM((parts, reach * block, width // parts), bf16),
+                pltpu.VMEM((parts, reach * block, width // parts), bf16),
+                pltpu.VMEM((rows, width), bf16),
+                pltpu.VMEM((rows, width), bf16),
+                pltpu.VMEM((parts, rows, width // parts), bf16),
+                pltpu.VMEM((parts, rows, width // parts), bf16),
+                pltpu.VMEM((parts, rows, width // parts), bf16),
+                pltpu.VMEM((parts, rows, width // parts), bf16),
+                pltpu.VMEM((rows, width // parts), f32),
                 pltpu.VMEM((rows, reach * block), bf16),
                 pltpu.VMEM((reach * block, rows), bf16),
                 pltpu.VMEM((rows, block), f32),
@@ -400,7 +558,6 @@
                 pltpu.VMEM((rows, width), f32),
                 pltpu.VMEM((rows, width), bf16),
                 pltpu.VMEM((rows, hidden), bf16),
-                pltpu.VMEM((2 * block, hidden), bf16),
                 pltpu.VMEM((rows, width), f32),
                 pltpu.SemaphoreType.DMA((5,)),
                 dma,
@@ -409,8 +566,16 @@
                 dma,
                 dma,
                 dma,
-                dma,
-                dma,
+                by_part,
+                by_part,
+                half,
+                half,
+                half,
+                half,
+                strip,
+                strip,
+                strip,
+                strip,
             ],
             compiler_params=pltpu.CompilerParams(
                 collective_id=0, has_side_effects=True, vmem_limit_bytes=60 * 1024 * 1024

time: 159 us -> 102 us (0.64)
  the two profiles are of different devices: /device:TPU:15 before, /device:TPU:3 now
where the time goes in v2:
time: 102 us; the launch traced here: 101 us
  Pallas kernels  93.3 us (91%)
  local copies, waits for them, and re-layouts  6.01 us (6%)
  between operations  1.29 us (1%)
    pallas_call x1, Pallas kernels, local(): pl.pallas_call(functools.partial(kernel, reach, group), out_shape=(jax.Sh...  93.3 us
    unnamed x2, local copies, waits for them, and re-layouts  3.74 us

profile of v2, /device:TPU:3, one launch (start us, length us, event | category | flops | bytes accessed | tf_op | source)
XLA Modules:
  0.0 101.3 jit_solution(5032011945342325231)
XLA Ops:
  1.3 0.1 pad.1.clone
  1.4 0.1 pad.2.clone
  1.4 0.7 bitcast_convert_fusion
  2.1 0.1 copy.12
  2.2 1.3 %copy.13.lists = s32[8,2]{1,0:T(8,128)} copy(s32[8,2]{0,1:T(2,128)} %bitcast.19) | data formatting | bytes 128 | tf_op jit(solution)/shard_map/squeeze | solution.py:512
  3.6 0.7 broadcast_in_dim.25.meta
  4.2 93.3 %shard_map.113 = (bf16[256,1024]{1,0:T(8,128)(2,1)}, bf16[256,1024]{1,0:T(8,128)(2,1)}) custom-call(s32[8,2]{1,0:T(8,128)} %copy.13.lists, s32[1,1]{1,0:T(1,128)S(6)} %copy.16.live, f32[8,8,128]{2,1,0:T(8,128)} %broadcast_in_dim.25.meta, bf16[256,1024]{1,0:T(8,128)(2,1)} %bitcast.15, f32[1,2048]{1,0:T(1,128)} %bitcast.17, f32[1,1024]{1,0:T(1,128)} %bitcast.18, ...), custom_call_target="tpu_custom_call" | custom-call | tf_op jit(solution)/shard_map/pallas_call | solution.py:526
  97.5 1.9 %copy.17 = bf16[1,256,1024]{2,1,0:T(8,128)(2,1)} copy(bf16[1,256,1024]{2,1,0:T(8,128)(2,1)} %bitcast.14) | data formatting | bytes 1048576
  99.4 1.9 %copy.18 = bf16[1,256,1024]{2,1,0:T(8,128)(2,1)} copy(bf16[1,256,1024]{2,1,0:T(8,128)(2,1)} %bitcast.13) | data formatting | bytes 1048576
  (2 shorter events, 0.0 us)

commit v3 on v2

--- a/solution.py
+++ b/solution.py
@@ -21,8 +21,6 @@
 def kernel(
     reach,
     group,
-    lists,
-    live,
     meta,
     feats,
     q_bias,
@@ -346,13 +344,13 @@
 
     lax.fori_loop(0, width // wide, add_pooled, 0)
     loads[4].wait()
-    own_live = live[0, 0]
+    own_live = meta[0][2:3, 0:1]
     chunk = 32
 
     def normalise(step, _):
         here = columns(step, chunk)
         pre = pre_act[here, :]
-        keep = (lax.broadcasted_iota(jnp.int32, (chunk, 1), 0) + step * chunk) < own_live
+        keep = (lax.broadcasted_iota(jnp.int32, (chunk, 1), 0) + step * chunk).astype(f32) < own_live
         activated = jnp.maximum(pre, 0.0)
         mean = jnp.sum(activated * activated, axis=1, keepdims=True) / width
         inv_norm = lax.rsqrt(mean + epsilon)
@@ -466,7 +464,7 @@
 
     def finish(step, _):
         here = columns(step, chunk)
-        keep = (lax.broadcasted_iota(jnp.int32, (chunk, 1), 0) + step * chunk) < own_live
+        keep = (lax.broadcasted_iota(jnp.int32, (chunk, 1), 0) + step * chunk).astype(f32) < own_live
         grads[here, :] = jnp.where(keep, total[here, :], 0.0).astype(bf16)
         return _
 
@@ -517,7 +515,6 @@
         columns = jnp.concatenate([flags, live, jnp.zeros((reach, 8 - block_count - 1), f32)], axis=1)
         meta = jnp.broadcast_to(columns[:, :, None], (reach, 8, lane))
         vmem = pl.BlockSpec(memory_space=pltpu.VMEM)
-        smem = pl.BlockSpec(memory_space=pltpu.SMEM)
         hbm = pl.BlockSpec(memory_space=pl.ANY)
         dma = pltpu.SemaphoreType.DMA((reach,))
         by_part = pltpu.SemaphoreType.DMA((parts, reach))
@@ -529,7 +526,7 @@
                 jax.ShapeDtypeStruct((rows, width), bf16),
                 jax.ShapeDtypeStruct((rows, width), bf16),
             ),
-            in_specs=[smem, smem, vmem, vmem, vmem, vmem, hbm, hbm, hbm, hbm, hbm],
+            in_specs=[vmem, vmem, vmem, vmem, hbm, hbm, hbm, hbm, hbm],
             out_specs=(vmem, vmem),
             scratch_shapes=[
                 pltpu.VMEM((rows, reach * rows), jnp.int32),
@@ -581,8 +578,6 @@
                 collective_id=0, has_side_effects=True, vmem_limit_bytes=60 * 1024 * 1024
             ),
         )(
-            lists,
-            live_rows,
             meta,
             features[0],
             q_bias.reshape(1, hidden),

time: 102 us -> 102 us (level)
  local copies, waits for them, and re-layouts: 6.01 us -> 4.67 us
    squeeze x1 -> x0, local copies, waits for them, and re-layouts: 1.34 us -> none  [local(): lists = listed[0, 0]]
where the time goes in v3:
time: 102 us; the launch traced here: 101 us
  Pallas kernels  94.1 us (92%)
  local copies, waits for them, and re-layouts  4.67 us (5%)
  between operations  1.29 us (1%)
    pallas_call x1, Pallas kernels, local(): pl.pallas_call(functools.partial(kernel, reach, group), out_shape=(jax.Sh...  94.1 us
    unnamed x2, local copies, waits for them, and re-layouts  3.74 us

profile of v3, /device:TPU:3, one launch (start us, length us, event | category | flops | bytes accessed | tf_op | source)
XLA Modules:
  0.0 100.8 jit_solution(17246605133409268098)
XLA Ops:
  1.3 0.1 pad.1.clone
  1.4 0.1 pad.2.clone
  1.4 0.7 convert_bitcast_fusion
  2.1 0.1 copy.12
  2.2 0.7 broadcast_in_dim.25.meta
  2.9 94.1 %shard_map.113 = (bf16[256,1024]{1,0:T(8,128)(2,1)}, bf16[256,1024]{1,0:T(8,128)(2,1)}) custom-call(f32[8,8,128]{2,1,0:T(8,128)} %broadcast_in_dim.25.meta, bf16[256,1024]{1,0:T(8,128)(2,1)} %bitcast.13, f32[1,2048]{1,0:T(1,128)} %bitcast.17, f32[1,1024]{1,0:T(1,128)} %bitcast.18, s32[256,2048]{1,0:T(8,128)} %bitcast.12, bf16[256,1024]{1,0:T(8,128)(2,1)} %bitcast.14, ...), custom_call_target="tpu_custom_call" | custom-call | tf_op jit(solution)/shard_map/pallas_call | solution.py:523
  97.0 1.9 %copy.16 = bf16[1,256,1024]{2,1,0:T(8,128)(2,1)} copy(bf16[1,256,1024]{2,1,0:T(8,128)(2,1)} %bitcast.16) | data formatting | bytes 1048576
  98.9 1.9 %copy.17 = bf16[1,256,1024]{2,1,0:T(8,128)(2,1)} copy(bf16[1,256,1024]{2,1,0:T(8,128)(2,1)} %bitcast.15) | data formatting | bytes 1048576
  (2 shorter events, 0.0 us)
